TPU v7x, 32 devices: a whole 2x2x4 slice. The times are simulated.
32 devices in a mesh: row: 8 (over z, x), col: 4 (over y, core).
Axes of the slice: x: 2, y: 2, z: 4, core: 2. Of those that a mesh axis runs over, the one named last changes fastest.
Arguments:
- features: bfloat16 [32768, 256], P(('col', 'row')), may hold values from -6 to 6
- adjacency: bfloat16 [256, 4, 12, 128, 128], P('row', 'col'), may hold values from 0 to 0.023925781
- block_cols: int32 [256, 4, 12], P('row', 'col'), may hold values from 0 to 63, as said below
- block_live: int32 [256, 4], P('row', 'col'), may hold values from 1 to 12, as said below
- weight: bfloat16 [256, 256], replicated, may hold values from -0.375 to 0.375
- bias: float32 [256], replicated, may hold values from -3 to 3
- upstream: bfloat16 [32768, 256], P(('row', 'col')), may hold values from -6 to 6
Outputs:
- activations: bfloat16 [32768, 256], P(('row', 'col'))
- feature_grad: bfloat16 [32768, 256], P(('col', 'row'))
- weight_grad: float32 [256, 256], replicated
- bias_grad: float32 [256], replicated
Inputs may be any that keep to these rules, and one draw needn't show every extreme that they name: `block_cols`: the live slots of one block row in one column tile name distinct column blocks of that tile. Slots k with k < block_live[i, c] are live; the other slots of block_cols and adjacency are ignored. Some entry equals 12.
All inputs are finite; a program needn't handle non-finite values.
Results may differ from a plain program's by a relative error of at most 0.014.
Values may be sent and summed in bfloat16 or wider, within the bound.
No kernel may reach another device: no remote copies, remote signals or barrier semaphores. Data moves between devices by JAX's collectives and lax.ppermute only.
A program may use at most 256 MiB of HBM per device.

v0:
```python
import jax
import jax.numpy as jnp
from jax import lax
from jax.sharding import PartitionSpec as P


def local(features, adjacency, block_cols, block_live, weight, bias, upstream):
    block_rows = adjacency.shape[0]
    block_slots = adjacency.shape[2]
    block_size = adjacency.shape[3]
    feature_width = features.shape[1]
    tile_blocks = adjacency.reshape(block_rows, block_slots, block_size, block_size)
    column_ids = block_cols.reshape(block_rows, block_slots)
    live_count = block_live.reshape(block_rows)
    live_mask = lax.broadcasted_iota(jnp.int32, (block_rows, block_slots), 1) < live_count[:, None]
    feature_panel = lax.all_gather(features, "row", axis=0, tiled=True)
    panel_blocks = feature_panel.shape[0] // block_size
    picked = feature_panel.reshape(panel_blocks, block_size, feature_width)[column_ids]
    picked = jnp.where(live_mask[:, :, None, None], picked, jnp.zeros((), jnp.bfloat16))
    partial_value = jnp.einsum(
        "ikab,ikbf->iaf", tile_blocks, picked, preferred_element_type=jnp.float32
    )
    partial_value = partial_value.reshape(block_rows * block_size, feature_width)
    aggregated = lax.psum_scatter(partial_value, "col", scatter_dimension=0, tiled=True).astype(
        jnp.bfloat16
    )
    preact = jnp.dot(aggregated, weight, preferred_element_type=jnp.float32) + bias
    sigmoid_pre = jax.nn.sigmoid(preact)
    outputs_here = (preact * sigmoid_pre).astype(jnp.bfloat16)
    derivative = sigmoid_pre * (1.0 + preact * (1.0 - sigmoid_pre))
    grad_pre = (upstream.astype(jnp.float32) * derivative).astype(jnp.bfloat16)
    weight_part = jnp.einsum("nf,ng->fg", aggregated, grad_pre, preferred_element_type=jnp.float32)
    bias_part = jnp.sum(grad_pre.astype(jnp.float32), axis=0)
    grad_agg = jnp.einsum("ng,fg->nf", grad_pre, weight, preferred_element_type=jnp.float32).astype(
        jnp.bfloat16
    )
    weight_grad, bias_grad = lax.psum((weight_part, bias_part), ("row", "col"))
    tile_grad = lax.all_gather(grad_agg, "col", axis=0, tiled=True)
    contrib = jnp.einsum(
        "ikab,iaf->ikbf",
        tile_blocks,
        tile_grad.reshape(block_rows, block_size, feature_width),
        preferred_element_type=jnp.float32,
    )
    contrib = contrib.reshape(block_rows * block_slots, block_size, feature_width)
    target_blocks = jnp.where(live_mask, column_ids, panel_blocks).reshape(-1)
    panel_sum = jnp.zeros((panel_blocks, block_size, feature_width), jnp.float32)
    panel_sum = panel_sum.at[target_blocks].add(contrib, mode="drop")
    panel_sum = panel_sum.reshape(panel_blocks * block_size, feature_width)
    feature_grad = lax.psum_scatter(
        panel_sum.astype(jnp.bfloat16), "row", scatter_dimension=0, tiled=True
    )
    return (outputs_here, feature_grad, weight_grad, bias_grad)


def solution(mesh):
    placed = (
        P(("col", "row"), None),
        P("row", "col", None, None, None),
        P("row", "col", None),
        P("row", "col"),
        P(),
        P(),
        P(("row", "col"), None),
    )
    return jax.shard_map(
        local,
        mesh=mesh,
        in_specs=placed,
        out_specs=(P(("row", "col"), None), P(("col", "row"), None), P(), P()),
        check_vma=False,
    )
```

profile of v0, /device:TPU:0, one launch (start us, length us, event | category | flops | bytes accessed | tf_op | source)
XLA Modules:
  0.0 477.4 jit_solution(3709703805803400464)
XLA Ops:
  7.2 0.0 copy-start
  7.2 0.0 all-gather.3.cloned.1.call-start
  7.2 0.7 all-gather.3.cloned.1.call-update
  7.9 0.0 reduce-scatter.3.cloned.1.call-start
  8.0 0.7 compare_select_fusion
  8.7 0.1 copy.12
  8.8 0.1 reshape.129
  8.9 0.7 iota_compare_fusion
  9.6 76.1 %all-gather.3.cloned.1.call-done = bf16[8192,256]{1,0:T(8,128)(2,1)} async-done(((bf16[1024,256]{1,0:T(8,128)(2,1)}), bf16[8192,256]{1,0:T(8,128)(2,1)}) %all-gather.3.cloned.1.call-update) | async-done | bytes 4194320 | tf_op jit(solution)/shard_map/all_gather | solution.py:16
  85.7 15.1 %gather_fusion = bf16[384,128,256]{2,1,0:T(8,128)(2,1)} fusion(bf16[64,128,256]{2,1,0:T(8,128)(2,1)} %bitcast.35, s32[1024]{0:T(1024)S(1)} %pad_clamp_fusion), kind=kCustom, calls=%fused_computation | custom fusion | bytes 50333184 | tf_op jit(solution)/shard_map/gather | solution.py:18
  100.8 0.0 copy-start.3
  100.8 0.0 copy-start.4
  100.8 16.1 %fusion = f32[32,256,128,1]{1,2,3,0:T(8,128)} fusion(bf16[32,12,128,256]{3,2,1,0:T(8,128)(2,1)} %bitcast.36, pred[32,12]{1,0:T(8,128)(4,1)S(1)} %iota_compare_fusion, bf16[32,1,12,128,128]{4,3,2,1,0:T(8,128)(2,1)} %param.8), kind=kOutput, calls=%fused_computation.2 | convolution fusion | flops 3233808384 | bytes 41943424 | tf_op jit(solution)/shard_map/ikab,ikbf->iaf/dot_general | solution.py:20
  116.9 0.0 copy-start.2
  116.9 0.0 reduce-scatter.3.cloned.1.call-update
  116.9 0.0 all-gather.5.cloned.1.call-start
  116.9 43.2 %reduce-scatter.3.cloned.1.call-done = f32[1024,256]{1,0:T(8,128)} async-done(((f32[4096,256]{1,0:T(8,128)}), f32[1024,256]{1,0:T(8,128)}) %reduce-scatter.3.cloned.1.call-update) | async-done | bytes 1048592 | tf_op jit(solution)/shard_map/reduce_scatter | solution.py:24
  160.2 0.0 copy-done
  160.2 0.0 copy-done.3
  160.2 0.0 copy-done.4
  160.2 2.7 convert_reduce_fusion
  162.9 1.1 convolution_convert_fusion
  164.0 0.0 all-gather.5.cloned.1.call-update
  164.0 0.0 all-reduce.2.cloned.1.call-start
  164.1 0.1 lt.53
  164.2 0.0 copy-done.2
  164.2 0.1 copy.13
  164.3 0.1 reshape.124
  164.4 2.3 fusion.7
  166.7 0.0 all-reduce.2.cloned.1.call-update
  166.7 0.0 reduce-scatter.5.cloned.1.call-start
  166.8 20.0 %all-gather.5.cloned.1.call-done = bf16[4096,256]{1,0:T(8,128)(2,1)} async-done(((bf16[1024,256]{1,0:T(8,128)(2,1)}), bf16[4096,256]{1,0:T(8,128)(2,1)}) %all-gather.5.cloned.1.call-update) | async-done | bytes 2097168 | tf_op jit(solution)/shard_map/all_gather | solution.py:38
  186.7 22.5 %fusion.3 = f32[32,256,12,128]{3,1,2,0:T(8,128)} fusion(bf16[32,128,256,1]{2,1,3,0:T(8,128)(2,1)} %bitcast.39, bf16[32,1,12,128,128]{4,3,2,1,0:T(8,128)(2,1)} %param.8), kind=kOutput, calls=%fused_computation.5 | convolution fusion | flops 3221225472 | bytes 65011712 | tf_op jit(solution)/shard_map/ikab,iaf->ikbf/dot_general | solution.py:39
  209.3 48.9 %copy.15 = f32[384,128,256]{2,1,0:T(8,128)} copy(f32[384,128,256]{1,2,0:T(8,128)} %bitcast.34) | data formatting | bytes 100663296 | tf_op jit(solution)/shard_map/reshape | solution.py:45
  258.2 4.2 broadcast_in_dim.23
  262.4 0.0 copy-start.1
  262.4 109.8 %scatter_fusion = f32[64,128,256]{2,1,0:T(8,128)} fusion(f32[64,128,256]{2,1,0:T(8,128)} %broadcast_in_dim.23, s32[384]{0:T(512)S(1)} %fusion.10, f32[384,128,256]{2,1,0:T(8,128)} %copy.15), kind=kCustom, calls=%fused_computation.1 | custom fusion | flops 12582912 | bytes 150996480 | tf_op jit(solution)/shard_map/scatter-add | solution.py:48
  372.2 5.9 %convert_element_type.29 = bf16[64,128,256]{2,1,0:T(8,128)(2,1)} convert(f32[64,128,256]{2,1,0:T(8,128)} %scatter_fusion) | non-fusion elementwise | flops 2097152 | bytes 12582912 | tf_op jit(solution)/shard_map/convert_element_type | solution.py:51
  378.1 0.0 reduce-scatter.5.cloned.1.call-update
  378.1 43.6 %psum.15 = f32[256]{0:T(256)} all-reduce(f32[256]{0:T(256)S(1)} %get-tuple-element.4), channel_id=1, replica_groups=mesh['row'=8,'col'=4] {'row','col'}, use_global_device_ids=true, to_apply=%region_5.6 | all-reduce | flops 256 | bytes 2048 | tf_op jit(solution)/shard_map/psum | solution.py:37
  421.8 0.0 all-reduce.2.cloned.1.call-done
  421.8 47.4 %reduce-scatter.5.cloned.1.call-done = bf16[1024,256]{1,0:T(8,128)(2,1)} async-done(((bf16[8192,256]{1,0:T(8,128)(2,1)}), bf16[1024,256]{1,0:T(8,128)(2,1)}) %reduce-scatter.5.cloned.1.call-update) | async-done | bytes 524304 | tf_op jit(solution)/shard_map/reduce_scatter | solution.py:50
  469.2 1.7 copy.22
  470.8 0.0 copy-done.1
  (2 shorter events, 0.0 us)
Async XLA Ops:
  7.2 153.0 %copy-start = (bf16[256,256]{1,0:T(8,128)(2,1)S(1)}, bf16[256,256]{1,0:T(8,128)(2,1)}, u32[]{:S(2)}) copy-start(bf16[256,256]{1,0:T(8,128)(2,1)} %param.11) | copy-start | bytes 393220
  7.2 78.5 %all-gather.3.cloned.1.call-start = ((), (), s32[]{:S(2)}) async-start(), calls=%async_computation.2 | async-start | bytes 4718592 | tf_op jit(solution)/shard_map/all_gather | solution.py:16
  7.9 152.3 %reduce-scatter.3.cloned.1.call-start = ((), (), s32[]{:S(2)}) async-start(), calls=%async_computation.3 | async-start | bytes 5242880 | tf_op jit(solution)/shard_map/reduce_scatter | solution.py:24
  100.8 59.4 %copy-start.3 = (bf16[1024,256]{1,0:T(8,128)(2,1)S(1)}, bf16[1024,256]{1,0:T(8,128)(2,1)}, u32[]{:S(2)}) copy-start(bf16[1024,256]{1,0:T(8,128)(2,1)} %param.13) | copy-start | bytes 1572868
  100.8 59.4 %copy-start.4 = (f32[256]{0:T(256)S(1)}, f32[256]{0:T(256)}, u32[]{:S(2)}) copy-start(f32[256]{0:T(256)} %param.12) | copy-start | bytes 3076
  116.9 47.3 %copy-start.2 = (s32[32,1,12]{0,1,2:T(1,128)S(1)}, s32[32,1,12]{0,1,2:T(1,128)}, u32[]{:S(2)}) copy-start(s32[32,1,12]{0,1,2:T(1,128)} %param.9) | copy-start | bytes 4612
  116.9 69.9 %all-gather.5.cloned.1.call-start = ((), (), s32[]{:S(2)}) async-start(), calls=%async_computation.4 | async-start | bytes 2621440 | tf_op jit(solution)/shard_map/all_gather | solution.py:38
  164.0 257.8 %all-reduce.2.cloned.1.call-start = ((), (), s32[]{:S(2)}) async-start(), calls=%async_computation.6 | async-start | bytes 524288 | tf_op jit(solution)/shard_map/psum | solution.py:37
  166.7 302.4 %reduce-scatter.5.cloned.1.call-start = ((), (), s32[]{:S(2)}) async-start(), calls=%async_computation.5 | async-start | bytes 4718592 | tf_op jit(solution)/shard_map/reduce_scatter | solution.py:50
  262.4 208.4 %copy-start.1 = (bf16[256,256]{1,0:T(8,128)(2,1)S(1)}, bf16[256,256]{1,0:T(8,128)(2,1)}, u32[]{:S(2)}) copy-start(bf16[256,256]{1,0:T(8,128)(2,1)} %param.11) | copy-start | bytes 393220
Sparse Core Ops, SparseCore 0:
  10.1 75.4 all-gather.2
  117.0 43.1 reduce-scatter.2
  164.2 22.5 all-gather.4
  192.7 126.5 all-reduce.1
  378.3 90.8 reduce-scatter.4
where the time goes:
time: 479 us; the launch traced here: 477 us
  waiting for transfers between devices  187 us (39%)
  other arithmetic  117 us (24%)
  local copies, waits for them, and re-layouts  70.4 us (15%)
  matrix products  44.7 us (9%)
  blocking collectives  43.6 us (9%)
  between operations  13.8 us (3%)
    scatter-add x1, other arithmetic, local(): panel_sum = panel_sum.at[target_blocks].add(contrib, mode='drop')  110 us
    all_gather x1, waiting for transfers between devices, local(): feature_panel = lax.all_gather(features, 'row', axis=0, tiled=True)  76.1 us
    reshape x1, local copies, waits for them, and re-layouts, local(): contrib.reshape(block_rows * block_slots, block_size, feature_width)  48.9 us
    reduce_scatter x1, waiting for transfers between devices, local(): lax.psum_scatter(panel_sum.astype(jnp.bfloat16), 'row', scatter_dimension...  47.4 us
    psum x1, blocking collectives, local(): weight_grad, bias_grad = lax.psum((weight_part, bias_part), ('row', 'col'))  43.6 us
    reduce_scatter x1, waiting for transfers between devices, local(): lax.psum_scatter(partial_value, 'col', scatter_dimension=0, tiled=True)  43.2 us
    dot_general x1, matrix products, local(): jnp.einsum('ikab,iaf->ikbf', tile_blocks, tile_grad.reshape(block_rows, b...  22.5 us
    all_gather x1, waiting for transfers between devices, local(): tile_grad = lax.all_gather(grad_agg, 'col', axis=0, tiled=True)  20 us
  transfers between devices with their start and end apart: 5, of which 4 were waited for; matrix products, arithmetic and copies ran while one was open for 41% of the time, Pallas kernels for 0%

commit v1 on v0

--- a/solution.py
+++ b/solution.py
@@ -2,6 +2,17 @@
 import jax.numpy as jnp
 from jax import lax
 from jax.sharding import PartitionSpec as P
+
+
+def pass_along(shard, axis, dim):
+    devices = lax.axis_size(axis)
+    right = [(i, (i + 1) % devices) for i in range(devices)]
+    parts = [shard]
+    for stride in range(1, devices):
+        parts = [lax.ppermute(parts[0], axis, right), *parts]
+    whole = jnp.concatenate(parts, axis=dim)
+    shift = (lax.axis_index(axis) + 1) * parts[-1].shape[dim]
+    return jnp.roll(whole, shift, axis=dim)
 
 
 def local(features, adjacency, block_cols, block_live, weight, bias, upstream):
@@ -13,7 +24,7 @@
     column_ids = block_cols.reshape(block_rows, block_slots)
     live_count = block_live.reshape(block_rows)
     live_mask = lax.broadcasted_iota(jnp.int32, (block_rows, block_slots), 1) < live_count[:, None]
-    feature_panel = lax.all_gather(features, "row", axis=0, tiled=True)
+    feature_panel = pass_along(features, "row", 0)
     panel_blocks = feature_panel.shape[0] // block_size
     picked = feature_panel.reshape(panel_blocks, block_size, feature_width)[column_ids]
     picked = jnp.where(live_mask[:, :, None, None], picked, jnp.zeros((), jnp.bfloat16))

time: 479 us -> 507 us (1.058)
  waiting for transfers between devices: 187 us -> 206 us
  local copies, waits for them, and re-layouts: 70.4 us -> 78.5 us
    ppermute x0 -> x7, waiting for transfers between devices: none -> 96.2 us  [pass_along(): parts = [lax.ppermute(parts[0], axis, right), *parts]]
    all_gather x1 -> x0, waiting for transfers between devices: 76.1 us -> none  [local(): feature_panel = lax.all_gather(features, 'row', axis=0, tiled=True)]
    unnamed x12 -> x31, local copies, waits for them, and re-layouts: 1.78 us -> 7.54 us
  transfers between devices with their start and end apart: 5 -> 11, of which waited for: 4 -> 10; matrix products, arithmetic and copies ran while one was open for 41% -> 38% of each run, Pallas kernels for 0% -> 0%
where the time goes in v1:
time: 507 us; the launch traced here: 506 us
  waiting for transfers between devices  206 us (41%)
  other arithmetic  116 us (23%)
  local copies, waits for them, and re-layouts  78.5 us (15%)
  blocking collectives  44.5 us (9%)
  matrix products  43.6 us (9%)
  between operations  14 us (3%)
    scatter-add x1, other arithmetic, local(): panel_sum = panel_sum.at[target_blocks].add(contrib, mode='drop')  109 us
    ppermute x7, waiting for transfers between devices, pass_along(): parts = [lax.ppermute(parts[0], axis, right), *parts]  96.2 us
    reshape x1, local copies, waits for them, and re-layouts, local(): contrib.reshape(block_rows * block_slots, block_size, feature_width)  48.9 us
    reduce_scatter x1, waiting for transfers between devices, local(): lax.psum_scatter(panel_sum.astype(jnp.bfloat16), 'row', scatter_dimension...  47.4 us
    psum x1, blocking collectives, local(): weight_grad, bias_grad = lax.psum((weight_part, bias_part), ('row', 'col'))  44.5 us
    reduce_scatter x1, waiting for transfers between devices, local(): lax.psum_scatter(partial_value, 'col', scatter_dimension=0, tiled=True)  41.1 us
    dot_general x1, matrix products, local(): jnp.einsum('ikab,iaf->ikbf', tile_blocks, tile_grad.reshape(block_rows, b...  22.5 us
    all_gather x1, waiting for transfers between devices, local(): tile_grad = lax.all_gather(grad_agg, 'col', axis=0, tiled=True)  21 us
  transfers between devices with their start and end apart: 11, of which 10 were waited for; matrix products, arithmetic and copies ran while one was open for 38% of the time, Pallas kernels for 0%

profile of v1, /device:TPU:0, one launch (start us, length us, event | category | flops | bytes accessed | tf_op | source)
XLA Modules:
  0.0 505.9 jit_solution(11586907400195535935)
XLA Ops:
  7.2 0.0 copy-start
  7.2 0.0 copy-start.2
  7.2 0.0 reduce-scatter.3.cloned.1.call-start
  7.2 3.0 collective-permute-start
  10.3 15.2 %collective-permute-done = bf16[1024,256]{1,0:T(8,128)(2,1)S(1)} collective-permute-done((bf16[1024,256]{1,0:T(8,128)(2,1)}, bf16[1024,256]{1,0:T(8,128)(2,1)S(1)}, u32[]{:S(2)}, u32[]{:S(2)}) %collective-permute-start) | collective-permute-done | bytes 524320 | tf_op jit(solution)/shard_map/ppermute | solution.py:12
  25.4 0.0 collective-permute-start.1
  25.4 15.8 %collective-permute-done.1 = bf16[1024,256]{1,0:T(8,128)(2,1)S(1)} collective-permute-done((bf16[1024,256]{1,0:T(8,128)(2,1)S(1)}, bf16[1024,256]{1,0:T(8,128)(2,1)S(1)}, u32[]{:S(2)}, u32[]{:S(2)}) %collective-permute-start.1) | collective-permute-done | bytes 524320 | tf_op jit(solution)/shard_map/ppermute | solution.py:12
  41.2 0.0 collective-permute-start.2
  41.2 14.9 %collective-permute-done.2 = bf16[1024,256]{1,0:T(8,128)(2,1)S(1)} collective-permute-done((bf16[1024,256]{1,0:T(8,128)(2,1)S(1)}, bf16[1024,256]{1,0:T(8,128)(2,1)S(1)}, u32[]{:S(2)}, u32[]{:S(2)}) %collective-permute-start.2) | collective-permute-done | bytes 524320 | tf_op jit(solution)/shard_map/ppermute | solution.py:12
  56.1 0.0 collective-permute-start.3
  56.2 14.1 %collective-permute-done.3 = bf16[1024,256]{1,0:T(8,128)(2,1)S(1)} collective-permute-done((bf16[1024,256]{1,0:T(8,128)(2,1)S(1)}, bf16[1024,256]{1,0:T(8,128)(2,1)S(1)}, u32[]{:S(2)}, u32[]{:S(2)}) %collective-permute-start.3) | collective-permute-done | bytes 524320 | tf_op jit(solution)/shard_map/ppermute | solution.py:12
  70.2 0.0 collective-permute-start.4
  70.2 13.2 %collective-permute-done.4 = bf16[1024,256]{1,0:T(8,128)(2,1)S(1)} collective-permute-done((bf16[1024,256]{1,0:T(8,128)(2,1)S(1)}, bf16[1024,256]{1,0:T(8,128)(2,1)S(1)}, u32[]{:S(2)}, u32[]{:S(2)}) %collective-permute-start.4) | collective-permute-done | bytes 524320 | tf_op jit(solution)/shard_map/ppermute | solution.py:12
  83.4 0.0 collective-permute-start.5
  83.4 12.5 %collective-permute-done.5 = bf16[1024,256]{1,0:T(8,128)(2,1)} collective-permute-done((bf16[1024,256]{1,0:T(8,128)(2,1)S(1)}, bf16[1024,256]{1,0:T(8,128)(2,1)}, u32[]{:S(2)}, u32[]{:S(2)}) %collective-permute-start.5) | collective-permute-done | bytes 524320 | tf_op jit(solution)/shard_map/ppermute | solution.py:12
  95.9 0.0 collective-permute-start.6
  95.9 0.7 compare_select_fusion
  96.6 0.1 copy.12
  96.7 0.1 reshape.129
  96.8 0.7 iota_compare_fusion
  97.6 10.5 %collective-permute-done.6 = bf16[1024,256]{1,0:T(8,128)(2,1)} collective-permute-done((bf16[1024,256]{1,0:T(8,128)(2,1)}, bf16[1024,256]{1,0:T(8,128)(2,1)}, u32[]{:S(2)}, u32[]{:S(2)}) %collective-permute-start.6) | collective-permute-done | bytes 524320 | tf_op jit(solution)/shard_map/ppermute | solution.py:12
  108.1 1.1 constant_dynamic-update-slice_fusion.15
  109.2 1.1 constant_dynamic-update-slice_fusion.14
  110.5 1.1 constant_dynamic-update-slice_fusion.8
  111.6 1.1 constant_dynamic-update-slice_fusion.7
  112.6 1.1 constant_dynamic-update-slice_fusion.6
  113.9 0.0 copy-done.2
  114.0 2.2 constant_dynamic-slice_fusion
  116.2 15.1 %gather_fusion = bf16[384,128,256]{2,1,0:T(8,128)(2,1)} fusion(bf16[64,128,256]{2,1,0:T(8,128)(2,1)} %bitcast.35, s32[1024]{0:T(1024)S(1)} %pad_clamp_fusion), kind=kCustom, calls=%fused_computation | custom fusion | bytes 50333184 | tf_op jit(solution)/shard_map/gather | solution.py:29
  131.4 0.0 copy-start.5
  131.4 0.0 copy-start.6
  131.4 16.1 %fusion = f32[32,256,128,1]{1,2,3,0:T(8,128)} fusion(bf16[32,12,128,256]{3,2,1,0:T(8,128)(2,1)} %bitcast.36, pred[32,12]{1,0:T(8,128)(4,1)S(1)} %iota_compare_fusion, bf16[32,1,12,128,128]{4,3,2,1,0:T(8,128)(2,1)} %param.8), kind=kOutput, calls=%fused_computation.2 | convolution fusion | flops 3233808384 | bytes 41943424 | tf_op jit(solution)/shard_map/ikab,ikbf->iaf/dot_general | solution.py:31
  147.5 0.0 copy-start.4
  147.5 0.0 reduce-scatter.3.cloned.1.call-update
  147.5 0.0 all-gather.2.cloned.1.call-start
  147.6 41.1 %reduce-scatter.3.cloned.1.call-done = f32[1024,256]{1,0:T(8,128)} async-done(((f32[4096,256]{1,0:T(8,128)}), f32[1024,256]{1,0:T(8,128)}) %reduce-scatter.3.cloned.1.call-update) | async-done | bytes 1048592 | tf_op jit(solution)/shard_map/reduce_scatter | solution.py:35
  188.6 0.0 copy-done
  188.6 0.0 copy-done.5
  188.6 0.0 copy-done.6
  188.6 0.0 copy-start.3
  188.6 2.8 convert_reduce_fusion
  191.4 1.1 convolution_convert_fusion
  192.5 0.0 all-gather.2.cloned.1.call-update
  192.6 0.0 all-reduce.2.cloned.1.call-start
  192.6 0.1 lt.67
  192.7 0.0 copy-done.4
  192.7 0.1 copy.13
  192.8 0.1 reshape.124
  193.0 0.0 copy-done.3
  193.0 1.0 fusion.7
  194.0 0.0 all-reduce.2.cloned.1.call-update
  194.0 0.2 reduce-scatter.5.cloned.1.call-start
  194.3 21.0 %all-gather.2.cloned.1.call-done = bf16[4096,256]{1,0:T(8,128)(2,1)} async-done(((bf16[1024,256]{1,0:T(8,128)(2,1)}), bf16[4096,256]{1,0:T(8,128)(2,1)}) %all-gather.2.cloned.1.call-update) | async-done | bytes 2097168 | tf_op jit(solution)/shard_map/all_gather | solution.py:49
  215.3 22.5 %fusion.3 = f32[32,256,12,128]{3,1,2,0:T(8,128)} fusion(bf16[32,128,256,1]{2,1,3,0:T(8,128)(2,1)} %bitcast.39, bf16[32,1,12,128,128]{4,3,2,1,0:T(8,128)(2,1)} %param.8), kind=kOutput, calls=%fused_computation.5 | convolution fusion | flops 3221225472 | bytes 65011712 | tf_op jit(solution)/shard_map/ikab,iaf->ikbf/dot_general | solution.py:50
  237.8 48.9 %copy.15 = f32[384,128,256]{2,1,0:T(8,128)} copy(f32[384,128,256]{1,2,0:T(8,128)} %bitcast.34) | data formatting | bytes 100663296 | tf_op jit(solution)/shard_map/reshape | solution.py:56
  286.7 4.3 broadcast_in_dim.23
  290.9 108.9 %scatter_fusion = f32[64,128,256]{2,1,0:T(8,128)} fusion(f32[64,128,256]{2,1,0:T(8,128)} %broadcast_in_dim.23, s32[384]{0:T(512)S(1)} %fusion.10, f32[384,128,256]{2,1,0:T(8,128)} %copy.15), kind=kCustom, calls=%fused_computation.1 | custom fusion | flops 12582912 | bytes 150996480 | tf_op jit(solution)/shard_map/scatter-add | solution.py:59
  399.8 5.9 %convert_element_type.29 = bf16[64,128,256]{2,1,0:T(8,128)(2,1)} convert(f32[64,128,256]{2,1,0:T(8,128)} %scatter_fusion) | non-fusion elementwise | flops 2097152 | bytes 12582912 | tf_op jit(solution)/shard_map/convert_element_type | solution.py:62
  405.7 0.0 reduce-scatter.5.cloned.1.call-update
  405.8 44.5 %psum.15 = f32[256]{0:T(256)} all-reduce(f32[256]{0:T(256)S(1)} %get-tuple-element.4), channel_id=1, replica_groups=mesh['row'=8,'col'=4] {'row','col'}, use_global_device_ids=true, to_apply=%region_5.6 | all-reduce | flops 256 | bytes 2048 | tf_op jit(solution)/shard_map/psum | solution.py:48
  450.3 0.0 all-reduce.2.cloned.1.call-done
  450.3 47.4 %reduce-scatter.5.cloned.1.call-done = bf16[1024,256]{1,0:T(8,128)(2,1)} async-done(((bf16[8192,256]{1,0:T(8,128)(2,1)}), bf16[1024,256]{1,0:T(8,128)(2,1)}) %reduce-scatter.5.cloned.1.call-update) | async-done | bytes 524304 | tf_op jit(solution)/shard_map/reduce_scatter | solution.py:61
  497.7 1.7 copy.37
  499.4 0.0 copy-done.1
  (14 shorter events, 0.4 us)
Async XLA Ops:
  7.2 181.5 %copy-start = (bf16[256,256]{1,0:T(8,128)(2,1)S(1)}, bf16[256,256]{1,0:T(8,128)(2,1)}, u32[]{:S(2)}) copy-start(bf16[256,256]{1,0:T(8,128)(2,1)} %param.11) | copy-start | bytes 393220
  7.2 106.8 %copy-start.2 = (bf16[1024,256]{1,0:T(8,128)(2,1)S(1)}, bf16[1024,256]{1,0:T(8,128)(2,1)}, u32[]{:S(2)}) copy-start(bf16[1024,256]{1,0:T(8,128)(2,1)} %param.7) | copy-start | bytes 1572868
  7.2 181.4 %reduce-scatter.3.cloned.1.call-start = ((), (), s32[]{:S(2)}) async-start(), calls=%async_computation.2 | async-start | bytes 5242880 | tf_op jit(solution)/shard_map/reduce_scatter | solution.py:35
  7.2 18.2 %collective-permute-start = (bf16[1024,256]{1,0:T(8,128)(2,1)}, bf16[1024,256]{1,0:T(8,128)(2,1)S(1)}, u32[]{:S(2)}, u32[]{:S(2)}) collective-permute-start(bf16[1024,256]{1,0:T(8,128)(2,1)} %param.7), channel_id=1, source_target_pairs={{0,4},{4,8},{8,12},{12,16},{16,20},{20,24},{24,28},{28,0},{1,5},{5... | collective-permute-start | bytes 1572872 | tf_op jit(solution)/shard_map/ppermute | solution.py:12
  25.4 15.8 %collective-permute-start.1 = (bf16[1024,256]{1,0:T(8,128)(2,1)S(1)}, bf16[1024,256]{1,0:T(8,128)(2,1)S(1)}, u32[]{:S(2)}, u32[]{:S(2)}) collective-permute-start(bf16[1024,256]{1,0:T(8,128)(2,1)S(1)} %collective-permute-done), channel_id=1, source_target_pairs={{0,4},{4,8},{8,12},{12,16},{16,20},{20,24},{24,28},{28,0},{1,5},{5... | collective-permute-start | bytes 1572872 | tf_op jit(solution)/shard_map/ppermute | solution.py:12
  41.2 14.9 %collective-permute-start.2 = (bf16[1024,256]{1,0:T(8,128)(2,1)S(1)}, bf16[1024,256]{1,0:T(8,128)(2,1)S(1)}, u32[]{:S(2)}, u32[]{:S(2)}) collective-permute-start(bf16[1024,256]{1,0:T(8,128)(2,1)S(1)} %collective-permute-done.1), channel_id=1, source_target_pairs={{0,4},{4,8},{8,12},{12,16},{16,20},{20,24},{24,28},{28,0},{1,5},{5... | collective-permute-start | bytes 1572872 | tf_op jit(solution)/shard_map/ppermute | solution.py:12
  56.1 14.1 %collective-permute-start.3 = (bf16[1024,256]{1,0:T(8,128)(2,1)S(1)}, bf16[1024,256]{1,0:T(8,128)(2,1)S(1)}, u32[]{:S(2)}, u32[]{:S(2)}) collective-permute-start(bf16[1024,256]{1,0:T(8,128)(2,1)S(1)} %collective-permute-done.2), channel_id=1, source_target_pairs={{0,4},{4,8},{8,12},{12,16},{16,20},{20,24},{24,28},{28,0},{1,5},{5... | collective-permute-start | bytes 1572872 | tf_op jit(solution)/shard_map/ppermute | solution.py:12
  70.2 13.2 %collective-permute-start.4 = (bf16[1024,256]{1,0:T(8,128)(2,1)S(1)}, bf16[1024,256]{1,0:T(8,128)(2,1)S(1)}, u32[]{:S(2)}, u32[]{:S(2)}) collective-permute-start(bf16[1024,256]{1,0:T(8,128)(2,1)S(1)} %collective-permute-done.3), channel_id=1, source_target_pairs={{0,4},{4,8},{8,12},{12,16},{16,20},{20,24},{24,28},{28,0},{1,5},{5... | collective-permute-start | bytes 1572872 | tf_op jit(solution)/shard_map/ppermute | solution.py:12
  83.4 12.5 %collective-permute-start.5 = (bf16[1024,256]{1,0:T(8,128)(2,1)S(1)}, bf16[1024,256]{1,0:T(8,128)(2,1)}, u32[]{:S(2)}, u32[]{:S(2)}) collective-permute-start(bf16[1024,256]{1,0:T(8,128)(2,1)S(1)} %collective-permute-done.4), channel_id=1, source_target_pairs={{0,4},{4,8},{8,12},{12,16},{16,20},{20,24},{24,28},{28,0},{1,5},{5... | collective-permute-start | bytes 1572872 | tf_op jit(solution)/shard_map/ppermute | solution.py:12
  95.9 12.2 %collective-permute-start.6 = (bf16[1024,256]{1,0:T(8,128)(2,1)}, bf16[1024,256]{1,0:T(8,128)(2,1)}, u32[]{:S(2)}, u32[]{:S(2)}) collective-permute-start(bf16[1024,256]{1,0:T(8,128)(2,1)} %collective-permute-done.5), channel_id=1, source_target_pairs={{0,4},{4,8},{8,12},{12,16},{16,20},{20,24},{24,28},{28,0},{1,5},{5... | collective-permute-start | bytes 1572872 | tf_op jit(solution)/shard_map/ppermute | solution.py:12
  131.4 57.3 %copy-start.5 = (bf16[1024,256]{1,0:T(8,128)(2,1)S(1)}, bf16[1024,256]{1,0:T(8,128)(2,1)}, u32[]{:S(2)}) copy-start(bf16[1024,256]{1,0:T(8,128)(2,1)} %param.13) | copy-start | bytes 1572868
  131.4 57.3 %copy-start.6 = (f32[256]{0:T(256)S(1)}, f32[256]{0:T(256)}, u32[]{:S(2)}) copy-start(f32[256]{0:T(256)} %param.12) | copy-start | bytes 3076
  147.5 45.3 %copy-start.4 = (s32[32,1,12]{0,1,2:T(1,128)S(1)}, s32[32,1,12]{0,1,2:T(1,128)}, u32[]{:S(2)}) copy-start(s32[32,1,12]{0,1,2:T(1,128)} %param.9) | copy-start | bytes 4612
  147.5 67.8 %all-gather.2.cloned.1.call-start = ((), (), s32[]{:S(2)}) async-start(), calls=%async_computation.3 | async-start | bytes 2621440 | tf_op jit(solution)/shard_map/all_gather | solution.py:49
  188.6 4.3 copy-start.3
  192.6 257.7 %all-reduce.2.cloned.1.call-start = ((), (), s32[]{:S(2)}) async-start(), calls=%async_computation.5 | async-start | bytes 524288 | tf_op jit(solution)/shard_map/psum | solution.py:48
  194.0 303.7 %reduce-scatter.5.cloned.1.call-start = ((), (), s32[]{:S(2)}) async-start(), calls=%async_computation.4 | async-start | bytes 4718592 | tf_op jit(solution)/shard_map/reduce_scatter | solution.py:61
  290.9 208.5 %copy-start.1 = (bf16[256,256]{1,0:T(8,128)(2,1)S(1)}, bf16[256,256]{1,0:T(8,128)(2,1)}, u32[]{:S(2)}) copy-start(bf16[256,256]{1,0:T(8,128)(2,1)} %param.11) | copy-start | bytes 393220
Sparse Core Ops, SparseCore 0:
  147.6 40.9 reduce-scatter.2
  192.7 22.5 all-gather.1
  221.4 126.5 all-reduce.1
  405.9 91.7 reduce-scatter.4
